TPU v7x, 32 devices: a whole 2x2x4 slice. The times are simulated.
32 devices in a mesh: row: 4 (over x, core), col: 8 (over z, y).
Axes of the slice: x: 2, y: 2, z: 4, core: 2. Of those that a mesh axis runs over, the one named last changes fastest.
Arguments:
- right_sides: float32 [3, 4, 512, 64], P(None, None, 'row'), may hold values from -6 to 6
- diag_inverse: float32 [3, 4, 512, 512], replicated, as said below
- sub_blocks: float32 [3, 4, 4, 512, 512], P(None, None, None, 'row', 'col'), may hold values from -0.125 to 0.125
- block_mask: int32 [3, 4, 4], replicated, may hold values 0 or 1
- anc_values: float32 [2, 4, 512, 512], P(None, None, 'row', 'col'), may hold values from -0.09375 to 0.09375
- anc_rows: int32 [2, 4, 512], P(None, None, 'row'), may hold values from 0 to 2047, as said below
- anc_count: int32 [2, 4], replicated, may hold values from 256 to 512, as said below
- far_factor: float32 [4, 512, 32768], P(None, 'col', 'row'), may hold values from -0.1875 to 0.1875
- far_rhs: float32 [32768, 64], P(('row', 'col')), may hold values from -6 to 6
- far_solution: float32 [32768, 64], P('row'), may hold values from -4 to 4
Outputs:
- forward_solution: float32 [3, 4, 512, 64], P(None, None, 'row')
- solution: float32 [3, 4, 512, 64], P(None, None, 'row')
- far_update: float32 [32768, 64], P(('row', 'col'))
Inputs may be any that keep to these rules, and one draw needn't show every extreme that they name: `diag_inverse`: each diagonal-block inverse is lower triangular. `anc_rows`: each list holds distinct rows of the parent's window in ascending order; entries at positions anc_count or later are not used. `anc_count`: some list is full and some holds exactly 256 live entries in every draw. `block_mask`: entries on and above the block diagonal are not used.
All inputs are finite; a program needn't handle non-finite values.
Results may differ from a plain program's by a relative error of at most 0.0001.
Values sent between devices are 32-bit elements; how exact they have to be, the bound alone decides.
A program may use at most 128 MiB of HBM per device.

v0:
```python
import jax
import jax.numpy as jnp
from jax import lax
from jax.sharding import PartitionSpec as P

FULL_PRECISION = lax.Precision.HIGHEST


def strict_lower(length):
    positions = jnp.arange(length)
    return (positions[:, None] > positions[None, :]).astype(jnp.float32)


def whole_forward(right_whole, inverse, lower_blocks, weights, extra, pair_of):
    panels = right_whole.shape[1]
    solved = []
    for panel_index in range(panels):
        residual = right_whole[:, panel_index] - extra[:, panel_index]
        for earlier in range(panel_index):
            block = lower_blocks[:, pair_of[panel_index, earlier]]
            term = jnp.einsum("bij,bjk->bik", block, solved[earlier], precision=FULL_PRECISION)
            residual = residual - term * weights[:, panel_index, earlier][:, None, None]
        solved.append(
            jnp.einsum("bij,bjk->bik", inverse[:, panel_index], residual, precision=FULL_PRECISION)
        )
    return jnp.stack(solved, axis=1)


def whole_backward(forward, inverse, lower_blocks, weights, extra, pair_of):
    panels = forward.shape[1]
    solved = [None] * panels
    for panel_index in reversed(range(panels)):
        residual = forward[:, panel_index] - extra[:, panel_index]
        for later in range(panel_index + 1, panels):
            block = lower_blocks[:, pair_of[later, panel_index]]
            term = jnp.einsum("bij,bik->bjk", block, solved[later], precision=FULL_PRECISION)
            residual = residual - term * weights[:, later, panel_index][:, None, None]
        solved[panel_index] = jnp.einsum(
            "bji,bjk->bik", inverse[:, panel_index], residual, precision=FULL_PRECISION
        )
    return jnp.stack(solved, axis=1)


def place_columns(local_term, col_start, width):
    shape = local_term.shape[:-2] + (width, local_term.shape[-1])
    return lax.dynamic_update_slice_in_dim(
        jnp.zeros(shape, jnp.float32), local_term, col_start, local_term.ndim - 2
    )


def on_device(
    right_sides,
    diag_inverse,
    sub_blocks,
    block_mask,
    anc_values,
    anc_rows,
    anc_count,
    far_factor,
    far_rhs,
    far_solution,
):
    row_width = right_sides.shape[2]
    col_width = sub_blocks.shape[4]
    columns = right_sides.shape[3]
    panels = diag_inverse.shape[1]
    width = diag_inverse.shape[2]
    row_start = lax.axis_index("row") * row_width
    col_start = lax.axis_index("col") * col_width
    kept_blocks = block_mask.astype(jnp.float32) * strict_lower(panels)[None]
    anc_width = anc_rows.shape[2]
    position = lax.axis_index("row") * anc_width + jnp.arange(anc_width)
    live_rows = (position[None, None, :] < anc_count[:, :, None]).astype(jnp.float32)
    pair_list_rows = [later for later in range(panels) for earlier in range(later)]
    pair_list_cols = [earlier for later in range(panels) for earlier in range(later)]
    pair_of = {}
    for pair_index in range(len(pair_list_rows)):
        pair_of[pair_list_rows[pair_index], pair_list_cols[pair_index]] = pair_index
    pair_rows = jnp.array(pair_list_rows, dtype=jnp.int32)
    pair_cols = jnp.array(pair_list_cols, dtype=jnp.int32)
    lower_local = sub_blocks[:, pair_rows, pair_cols]
    lower_part = lax.all_gather(lower_local, "row", axis=2, tiled=True)
    lower_blocks = lax.all_gather(lower_part, "col", axis=3, tiled=True)
    right_whole = lax.all_gather(right_sides, "row", axis=2, tiled=True)
    zero_extra = jnp.zeros((2, panels, width, columns), jnp.float32)
    child_forward = whole_forward(
        right_whole[:2], diag_inverse[:2], lower_blocks[:2], kept_blocks[:2], zero_extra, pair_of
    )
    child_cols = lax.dynamic_slice_in_dim(child_forward, col_start, col_width, 2)
    updates = jnp.einsum("spaj,spjk->spak", anc_values, child_cols, precision=FULL_PRECISION)
    updates = updates * live_rows[..., None]
    spread = (
        jnp.zeros((panels * width, columns), jnp.float32)
        .at[anc_rows.reshape(-1)]
        .add(updates.reshape(-1, columns))
    )
    ancestor = lax.psum(spread, ("row", "col")).reshape(panels, width, columns)
    parent_forward = whole_forward(
        right_whole[2:],
        diag_inverse[2:],
        lower_blocks[2:],
        kept_blocks[2:],
        ancestor[None],
        pair_of,
    )
    parent_cols = lax.dynamic_slice_in_dim(parent_forward[0], col_start, col_width, 1)
    far_update = far_rhs - lax.psum_scatter(
        jnp.einsum("pjr,pjk->rk", far_factor, parent_cols, precision=FULL_PRECISION),
        "col",
        scatter_dimension=0,
        tiled=True,
    )
    far_back = jnp.einsum("pjr,rk->pjk", far_factor, far_solution, precision=FULL_PRECISION)
    far_whole = lax.psum(place_columns(far_back, col_start, width), ("row", "col"))
    parent_solution = whole_backward(
        parent_forward,
        diag_inverse[2:],
        lower_blocks[2:],
        kept_blocks[2:],
        far_whole[None],
        pair_of,
    )
    parent_flat = parent_solution[0].reshape(panels * width, columns)
    picked = parent_flat[anc_rows] * live_rows[..., None]
    child_extra = jnp.einsum("spaj,spak->spjk", anc_values, picked, precision=FULL_PRECISION)
    extra_whole = lax.psum(place_columns(child_extra, col_start, width), ("row", "col"))
    child_solution = whole_backward(
        child_forward, diag_inverse[:2], lower_blocks[:2], kept_blocks[:2], extra_whole, pair_of
    )
    forward_all = jnp.concatenate([child_forward, parent_forward], axis=0)
    solution_all = jnp.concatenate([child_solution, parent_solution], axis=0)
    forward_rows = lax.dynamic_slice_in_dim(forward_all, row_start, row_width, 2)
    solution_rows = lax.dynamic_slice_in_dim(solution_all, row_start, row_width, 2)
    return (forward_rows, solution_rows, far_update)


def solution(mesh):
    in_specs = (
        P(None, None, "row", None),
        P(),
        P(None, None, None, "row", "col"),
        P(),
        P(None, None, "row", "col"),
        P(None, None, "row"),
        P(),
        P(None, "col", "row"),
        P(("row", "col"), None),
        P("row", None),
    )
    out_specs = (P(None, None, "row", None), P(None, None, "row", None), P(("row", "col"), None))
    return jax.shard_map(
        on_device, mesh=mesh, in_specs=in_specs, out_specs=out_specs, check_vma=False
    )
```

profile of v0, /device:TPU:0, one launch (start us, length us, event | category | flops | bytes accessed | tf_op | source)
XLA Modules:
  0.0 859.8 jit_solution(2775651494124286492)
XLA Ops:
  7.2 3.1 gather_fusion
  12.3 25.3 %all-gather.6.cloned.1.call-done = f32[3,6,512,64]{2,3,0,1:T(8,128)} async-done(((f32[3,6,128,64]{2,3,0,1:T(8,128)}), f32[3,6,512,64]{2,3,0,1:T(8,128)}) %all-gather.6.cloned.1.call-update) | async-done | bytes 2359312 | tf_op jit(solution)/shard_map/all_gather | solution.py:82
  37.6 3.3 copy.100
  41.8 14.5 %fusion.66 = f32[1,4,64,64]{2,3,1,0:T(8,128)S(1)} fusion(f32[4,64,8192]{2,1,0:T(8,128)} %param.19, f32[8192,64]{0,1:T(8,128)S(1)} %copy-done), kind=kOutput, calls=%fused_computation.86 | convolution fusion | flops 1610612736 | bytes 10551296 | tf_op jit(solution)/shard_map/pjr,rk->pjk/dot_general | solution.py:113
  59.6 3.7 fusion.14
  63.3 360.3 %all-gather.8.cloned.1.call-done = f32[3,6,512,512]{2,3,1,0:T(8,128)} async-done(((f32[3,6,512,64]{2,3,1,0:T(8,128)}), f32[3,6,512,512]{2,3,1,0:T(8,128)}) %all-gather.8.cloned.1.call-update) | async-done | bytes 18874384 | tf_op jit(solution)/shard_map/all_gather | solution.py:83
  423.6 3.1 fusion.59
  426.7 3.7 fusion.10
  436.5 3.7 fusion.6
  446.3 3.3 fusion.39
  449.6 3.7 fusion.2
  454.0 6.3 scatter_custom_fusion
  462.1 129.6 %all-reduce.6.cloned.1.call-done = (f32[1,4,512,64]{2,3,1,0:T(8,128)}, f32[1,4,512,64]{2,3,1,0:T(8,128)}) async-done(((f32[1,4,512,64]{2,3,1,0:T(8,128)}, f32[1,4,512,64]{2,3,1,0:T(8,128)}), (f32[1,4,512,64]{2,3,1,0:T(8,128)}, f32[1,4,512,64]{2,3,1,0:T(8,128)})) %all-reduce.6.cloned.1.call-update) | async-done | bytes 1048592 | tf_op jit(solution)/shard_map/psum | solution.py:97
  632.3 3.5 convolution_multiply_fusion.1
  651.3 8.9 %convolution_bitcast_fusion = f32[8192,64]{0,1:T(8,128)} fusion(f32[4,64,8192]{2,1,0:T(8,128)} %param.19, f32[1,4,512,64]{2,3,1,0:T(8,128)S(1)} %get-tuple-element.26, s32[]{:T(128)S(6)} %select_n.32), kind=kOutput, calls=%fused_computation.3 | convolution fusion | flops 1610612736 | bytes 10616836 | tf_op jit(solution)/shard_map/pjr,pjk->rk/dot_general | solution.py:108
  660.3 120.1 %all-reduce.4.cloned.1.call-done = f32[2,4,512,64]{2,3,0,1:T(8,128)} async-done(((f32[2,4,512,64]{2,3,0,1:T(8,128)}), f32[2,4,512,64]{2,3,0,1:T(8,128)}) %all-reduce.4.cloned.1.call-update) | async-done | bytes 1048592 | tf_op jit(solution)/shard_map/psum | solution.py:126
  783.5 3.8 fusion.41
  787.4 3.1 fusion.4
  790.5 3.8 fusion.53
  794.3 3.8 fusion.45
  801.1 3.8 fusion.61
  804.9 3.8 fusion.57
  808.7 3.8 fusion.49
  817.1 33.9 %reduce-scatter.2.cloned.1.call-done = f32[1024,64]{0,1:T(8,128)} async-done(((f32[8192,64]{0,1:T(8,128)}), f32[1024,64]{0,1:T(8,128)}) %reduce-scatter.2.cloned.1.call-update) | async-done | bytes 262160 | tf_op jit(solution)/shard_map/reduce_scatter | solution.py:107
  (105 shorter events, 89.2 us)
Async XLA Ops:
  7.2 34.6 %copy-start = (f32[8192,64]{0,1:T(8,128)S(1)}, f32[8192,64]{0,1:T(8,128)}, u32[]{:S(2)}) copy-start(f32[8192,64]{0,1:T(8,128)} %param.21) | copy-start | bytes 6291460
  7.2 49.8 %copy-start.10 = (s32[3,4,4]{2,1,0:T(4,128)S(1)}, s32[3,4,4]{2,1,0:T(4,128)}, u32[]{:S(2)}) copy-start(s32[3,4,4]{2,1,0:T(4,128)} %param.15) | copy-start | bytes 580
  7.2 50.0 %copy-start.9 = (s32[2,4,128]{2,1,0:T(4,128)S(1)}, s32[2,4,128]{2,1,0:T(4,128)}, u32[]{:S(2)}) copy-start(s32[2,4,128]{2,1,0:T(4,128)} %param.17) | copy-start | bytes 12292
  7.2 30.4 %all-gather.6.cloned.1.call-start = ((), (), s32[]{:S(2)}) async-start(), calls=%async_computation.2 | async-start | bytes 2949120 | tf_op jit(solution)/shard_map/all_gather | solution.py:82
  10.4 49.2 %all-gather.4.cloned.1.call-start = ((), (), s32[]{:S(2)}) async-start(), calls=%async_computation.1 | async-start | bytes 1966080 | tf_op jit(solution)/shard_map/all_gather | solution.py:84
  12.2 411.4 %all-gather.8.cloned.1.call-start = ((), (), s32[]{:S(2)}) async-start(), calls=%async_computation.3 | async-start | bytes 21233664 | tf_op jit(solution)/shard_map/all_gather | solution.py:83
  40.9 550.8 %all-reduce.6.cloned.1.call-start = ((), (), s32[]{:S(2)}) async-start(), calls=%async_computation.6 | async-start | bytes 2097152 | tf_op jit(solution)/shard_map/psum | solution.py:97
  57.0 392.6 %copy-start.5 = (f32[1,4,512,64]{2,3,1,0:T(8,128)}, f32[1,4,512,64]{2,3,1,0:T(8,128)S(1)}, u32[]{:S(2)}) copy-start(f32[1,4,512,64]{2,3,1,0:T(8,128)S(1)} %dynamic_update_slice.8) | copy-start | bytes 1572868
  57.2 392.4 %copy-start.11 = (f32[2]{0:T(128)}, f32[2]{0:T(128)S(1)}, u32[]{:S(2)}) copy-start(f32[2]{0:T(128)S(1)} %get-tuple-element.19) | copy-start | bytes 28
  57.2 392.4 %copy-start.13 = (f32[2]{0:T(128)}, f32[2]{0:T(128)S(1)}, u32[]{:S(2)}) copy-start(f32[2]{0:T(128)S(1)} %get-tuple-element.23) | copy-start | bytes 28
  57.2 392.4 %copy-start.15 = (f32[2]{0:T(128)}, f32[2]{0:T(128)S(1)}, u32[]{:S(2)}) copy-start(f32[2]{0:T(128)S(1)} %get-tuple-element.21) | copy-start | bytes 28
  57.2 392.4 %copy-start.17 = (f32[2]{0:T(128)}, f32[2]{0:T(128)S(1)}, u32[]{:S(2)}) copy-start(f32[2]{0:T(128)S(1)} %get-tuple-element.18) | copy-start | bytes 28
  423.6 29.7 %copy-start.6 = (f32[2,4,128,64]{2,3,1,0:T(8,128)S(1)}, f32[2,4,128,64]{2,3,1,0:T(8,128)}, u32[]{:S(2)}) copy-start(f32[2,4,128,64]{2,3,1,0:T(8,128)} %param.16) | copy-start | bytes 786436
  461.4 319.0 %all-reduce.4.cloned.1.call-start = ((), (), s32[]{:S(2)}) async-start(), calls=%async_computation.4 | async-start | bytes 2097152 | tf_op jit(solution)/shard_map/psum | solution.py:126
  591.7 25.7 %copy-start.7 = (f32[1,4,512,64]{2,3,1,0:T(8,128)S(1)}, f32[1,4,512,64]{2,3,1,0:T(8,128)}, u32[]{:S(2)}) copy-start(f32[1,4,512,64]{2,3,1,0:T(8,128)} %get-tuple-element.25) | copy-start | bytes 1572868
  645.0 138.5 %copy-start.18 = (f32[2]{0:T(128)S(1)}, f32[2]{0:T(128)}, u32[]{:S(2)}) copy-start(f32[2]{0:T(128)} %copy-done.17) | copy-start | bytes 28
  648.6 142.0 %copy-start.16 = (f32[2]{0:T(128)S(1)}, f32[2]{0:T(128)}, u32[]{:S(2)}) copy-start(f32[2]{0:T(128)} %copy-done.15) | copy-start | bytes 28
  650.3 200.7 %reduce-scatter.2.cloned.1.call-start = ((), (), s32[]{:S(2)}) async-start(), calls=%async_computation.5 | async-start | bytes 2359296 | tf_op jit(solution)/shard_map/reduce_scatter | solution.py:107
  651.3 143.0 %copy-start.12 = (f32[2]{0:T(128)S(1)}, f32[2]{0:T(128)}, u32[]{:S(2)}) copy-start(f32[2]{0:T(128)} %copy-done.11) | copy-start | bytes 28
  651.3 149.8 %copy-start.14 = (f32[2]{0:T(128)S(1)}, f32[2]{0:T(128)}, u32[]{:S(2)}) copy-start(f32[2]{0:T(128)} %copy-done.13) | copy-start | bytes 28
  783.5 31.9 %copy-start.3 = (f32[1,4,512,64]{2,3,0,1:T(8,128)S(1)}, f32[1,4,512,64]{2,3,0,1:T(8,128)}, u32[]{:S(2)}) copy-start(f32[1,4,512,64]{2,3,0,1:T(8,128)} %get-tuple-element.28) | copy-start | bytes 1572868
  783.5 31.9 %copy-start.4 = (f32[1,4,512,64]{2,3,0,1:T(8,128)S(1)}, f32[1,4,512,64]{2,3,0,1:T(8,128)}, u32[]{:S(2)}) copy-start(f32[1,4,512,64]{2,3,0,1:T(8,128)} %get-tuple-element.27) | copy-start | bytes 1572868
  787.4 65.4 %copy-start.1 = (f32[8192,64]{0,1:T(8,128)S(1)}, f32[8192,64]{0,1:T(8,128)}, u32[]{:S(2)}) copy-start(f32[8192,64]{0,1:T(8,128)} %param.21) | copy-start | bytes 6291460
  790.5 60.5 %copy-start.8 = (f32[1024,64]{0,1:T(8,128)S(1)}, f32[1024,64]{0,1:T(8,128)}, u32[]{:S(2)}) copy-start(f32[1024,64]{0,1:T(8,128)} %param.20) | copy-start | bytes 786436
  (1 other events, 1.0 us)
Sparse Core Ops, SparseCore 0:
  10.5 27.0 all-gather.5
  39.7 19.8 all-gather.3
  61.1 362.4 all-gather.7
  461.5 130.1 all-reduce.5
  650.4 129.9 all-reduce.3
  783.8 67.1 reduce-scatter.1
where the time goes:
time: 866 us; the launch traced here: 860 us
  waiting for transfers between devices  672 us (78%)
  matrix products  145 us (17%)
  local copies, waits for them, and re-layouts  17.7 us (2%)
  between operations  14.7 us (2%)
  other arithmetic  10.7 us (1%)
    all_gather x1, waiting for transfers between devices, on_device(): lower_blocks = lax.all_gather(lower_part, 'col', axis=3, tiled=True)  360 us
    psum x1, waiting for transfers between devices, on_device(): ancestor = lax.psum(spread, ('row', 'col')).reshape(panels, width, columns)  130 us
    psum x1, waiting for transfers between devices, on_device(): lax.psum(place_columns(child_extra, col_start, width), ('row', 'col'))  120 us
    dot_general x12, matrix products, whole_backward(): jnp.einsum('bij,bik->bjk', block, solved[later], precision=FULL_PRECISION)  41.1 us
    dot_general x12, matrix products, whole_forward(): jnp.einsum('bij,bjk->bik', block, solved[earlier], precision=FULL_PRECISION)  34.6 us
    reduce_scatter x1, waiting for transfers between devices, on_device(): lax.psum_scatter(jnp.einsum('pjr,pjk->rk', far_factor, parent_cols, preci...  33.9 us
    all_gather x1, waiting for transfers between devices, on_device(): lower_part = lax.all_gather(lower_local, 'row', axis=2, tiled=True)  25.3 us
    dot_general x8, matrix products, whole_forward(): jnp.einsum('bij,bjk->bik', inverse[:, panel_index], residual, precision=F...  24.4 us
  transfers between devices with their start and end apart: 6, of which 6 were waited for; matrix products, arithmetic and copies ran while one was open for 8% of the time, Pallas kernels for 0%

commit v1 on v0

--- a/solution.py
+++ b/solution.py
@@ -123,7 +123,9 @@
     parent_flat = parent_solution[0].reshape(panels * width, columns)
     picked = parent_flat[anc_rows] * live_rows[..., None]
     child_extra = jnp.einsum("spaj,spak->spjk", anc_values, picked, precision=FULL_PRECISION)
-    extra_whole = lax.psum(place_columns(child_extra, col_start, width), ("row", "col"))
+    extra_whole = jnp.sum(
+        lax.all_gather(place_columns(child_extra, col_start, width), ("row", "col")), axis=0
+    )
     child_solution = whole_backward(
         child_forward, diag_inverse[:2], lower_blocks[:2], kept_blocks[:2], extra_whole, pair_of
     )

time: 866 us -> 954 us (1.10)
  waiting for transfers between devices: 672 us -> 748 us
  other arithmetic: 10.7 us -> 22.5 us
    all_gather x0 -> x1, waiting for transfers between devices: none -> 195 us  [on_device(): lax.all_gather(place_columns(child_extra, col_start, width), ('row', 'col'))]
    psum x1 -> x0, waiting for transfers between devices: 120 us -> none  [on_device(): lax.psum(place_columns(child_extra, col_start, width), ('row', 'col'))]
    reduce_sum x0 -> x1, other arithmetic: none -> 12.5 us  [on_device(): jnp.sum(lax.all_gather(place_columns(child_extra, col_start, width), ('ro...]
  transfers between devices with their start and end apart: 6 -> 6, of which waited for: 6 -> 6; matrix products, arithmetic and copies ran while one was open for 8% -> 6% of each run, Pallas kernels for 0% -> 0%
where the time goes in v1:
time: 954 us; the launch traced here: 948 us
  waiting for transfers between devices  748 us (78%)
  matrix products  145 us (15%)
  other arithmetic  22.5 us (2%)
  local copies, waits for them, and re-layouts  17.7 us (2%)
  between operations  14.7 us (2%)
    all_gather x1, waiting for transfers between devices, on_device(): lower_blocks = lax.all_gather(lower_part, 'col', axis=3, tiled=True)  360 us
    all_gather x1, waiting for transfers between devices, on_device(): lax.all_gather(place_columns(child_extra, col_start, width), ('row', 'col'))  195 us
    psum x1, waiting for transfers between devices, on_device(): ancestor = lax.psum(spread, ('row', 'col')).reshape(panels, width, columns)  130 us
    dot_general x12, matrix products, whole_backward(): jnp.einsum('bij,bik->bjk', block, solved[later], precision=FULL_PRECISION)  40.7 us
    dot_general x12, matrix products, whole_forward(): jnp.einsum('bij,bjk->bik', block, solved[earlier], precision=FULL_PRECISION)  34.8 us
    reduce_scatter x1, waiting for transfers between devices, on_device(): lax.psum_scatter(jnp.einsum('pjr,pjk->rk', far_factor, parent_cols, preci...  34.5 us
    all_gather x1, waiting for transfers between devices, on_device(): lower_part = lax.all_gather(lower_local, 'row', axis=2, tiled=True)  25.3 us
    dot_general x8, matrix products, whole_forward(): jnp.einsum('bij,bjk->bik', inverse[:, panel_index], residual, precision=F...  24.4 us
  transfers between devices with their start and end apart: 6, of which 6 were waited for; matrix products, arithmetic and copies ran while one was open for 6% of the time, Pallas kernels for 0%

profile of v1, /device:TPU:0, one launch (start us, length us, event | category | flops | bytes accessed | tf_op | source)
XLA Modules:
  0.0 948.3 jit_solution(2089855624483810125)
XLA Ops:
  7.3 3.1 gather_fusion
  12.3 25.3 %all-gather.7.cloned.1.call-done = f32[3,6,512,64]{2,3,0,1:T(8,128)} async-done(((f32[3,6,128,64]{2,3,0,1:T(8,128)}), f32[3,6,512,64]{2,3,0,1:T(8,128)}) %all-gather.7.cloned.1.call-update) | async-done | bytes 2359312 | tf_op jit(solution)/shard_map/all_gather | solution.py:82
  37.6 3.4 copy.94
  41.0 14.5 %fusion.66 = f32[1,4,64,64]{2,3,1,0:T(8,128)S(1)} fusion(f32[4,64,8192]{2,1,0:T(8,128)} %param.19, f32[8192,64]{0,1:T(8,128)S(1)} %copy-done), kind=kOutput, calls=%fused_computation.86 | convolution fusion | flops 1610612736 | bytes 10551296 | tf_op jit(solution)/shard_map/pjr,rk->pjk/dot_general | solution.py:113
  59.6 3.7 fusion.14
  63.3 360.3 %all-gather.9.cloned.1.call-done = f32[3,6,512,512]{2,3,1,0:T(8,128)} async-done(((f32[3,6,512,64]{2,3,1,0:T(8,128)}), f32[3,6,512,512]{2,3,1,0:T(8,128)}) %all-gather.9.cloned.1.call-update) | async-done | bytes 18874384 | tf_op jit(solution)/shard_map/all_gather | solution.py:83
  426.7 3.7 fusion.10
  436.5 3.7 fusion.6
  446.3 3.2 fusion.39
  449.6 3.7 fusion.2
  454.0 6.3 scatter_custom_fusion
  462.1 129.5 %all-reduce.3.cloned.1.call-done = (f32[1,4,512,64]{2,3,1,0:T(8,128)}, f32[1,4,512,64]{2,3,1,0:T(8,128)}) async-done(((f32[1,4,512,64]{2,3,1,0:T(8,128)}, f32[1,4,512,64]{2,3,1,0:T(8,128)}), (f32[1,4,512,64]{2,3,1,0:T(8,128)}, f32[1,4,512,64]{2,3,1,0:T(8,128)})) %all-reduce.3.cloned.1.call-update) | async-done | bytes 1048592 | tf_op jit(solution)/shard_map/psum | solution.py:97
  618.4 9.2 convolution_bitcast_fusion
  660.3 34.5 %reduce-scatter.2.cloned.1.call-done = f32[1024,64]{0,1:T(8,128)} async-done(((f32[8192,64]{0,1:T(8,128)}), f32[1024,64]{0,1:T(8,128)}) %reduce-scatter.2.cloned.1.call-update) | async-done | bytes 262160 | tf_op jit(solution)/shard_map/reduce_scatter | solution.py:107
  696.5 195.5 %all-gather.11.cloned.1.call-done = f32[32,2,4,512,64]{3,4,2,1,0:T(8,128)} async-done(((f32[1,2,4,512,64]{3,4,2,1,0:T(8,128)}), f32[32,2,4,512,64]{3,4,2,1,0:T(8,128)}) %all-gather.11.cloned.1.call-update) | async-done | bytes 33554448 | tf_op jit(solution)/shard_map/all_gather | solution.py:127
  892.0 12.5 %reduce_sum.9 = f32[2,4,512,64]{2,3,1,0:T(8,128)S(1)} reduce(f32[32,2,4,512,64]{3,4,2,1,0:T(8,128)} %all-gather.11.cloned.1.call-done, f32[]{:T(128)} %constant.13.clone.1), dimensions={0}, to_apply=%region_3.0 | reduce | flops 8126464 | bytes 34603012 | tf_op jit(solution)/shard_map/reduce_sum | solution.py:126
  904.5 3.4 fusion
  907.9 3.8 fusion.41
  911.7 3.1 fusion.4
  914.9 3.8 fusion.53
  918.6 3.7 fusion.45
  925.4 3.8 fusion.61
  929.1 3.7 fusion.57
  932.9 3.7 fusion.49
  (91 shorter events, 92.5 us)
Async XLA Ops:
  7.2 33.9 %copy-start = (f32[8192,64]{0,1:T(8,128)S(1)}, f32[8192,64]{0,1:T(8,128)}, u32[]{:S(2)}) copy-start(f32[8192,64]{0,1:T(8,128)} %param.21) | copy-start | bytes 6291460
  7.2 49.1 %copy-start.10 = (s32[3,4,4]{2,1,0:T(4,128)S(1)}, s32[3,4,4]{2,1,0:T(4,128)}, u32[]{:S(2)}) copy-start(s32[3,4,4]{2,1,0:T(4,128)} %param.15) | copy-start | bytes 580
  7.2 49.3 %copy-start.11 = (s32[2,4]{1,0:T(2,128)S(1)}, s32[2,4]{1,0:T(2,128)}, u32[]{:S(2)}) copy-start(s32[2,4]{1,0:T(2,128)} %param.18) | copy-start | bytes 100
  7.2 49.4 %copy-start.9 = (s32[2,4,128]{2,1,0:T(4,128)S(1)}, s32[2,4,128]{2,1,0:T(4,128)}, u32[]{:S(2)}) copy-start(s32[2,4,128]{2,1,0:T(4,128)} %param.17) | copy-start | bytes 12292
  7.2 30.4 %all-gather.7.cloned.1.call-start = ((), (), s32[]{:S(2)}) async-start(), calls=%async_computation.2 | async-start | bytes 2949120 | tf_op jit(solution)/shard_map/all_gather | solution.py:82
  10.4 49.2 %all-gather.5.cloned.1.call-start = ((), (), s32[]{:S(2)}) async-start(), calls=%async_computation.1 | async-start | bytes 1966080 | tf_op jit(solution)/shard_map/all_gather | solution.py:84
  12.2 411.4 %all-gather.9.cloned.1.call-start = ((), (), s32[]{:S(2)}) async-start(), calls=%async_computation.3 | async-start | bytes 21233664 | tf_op jit(solution)/shard_map/all_gather | solution.py:83
  41.0 550.7 %all-reduce.3.cloned.1.call-start = ((), (), s32[]{:S(2)}) async-start(), calls=%async_computation.6 | async-start | bytes 2097152 | tf_op jit(solution)/shard_map/psum | solution.py:97
  56.3 393.3 %copy-start.6 = (f32[1,4,512,64]{2,3,1,0:T(8,128)}, f32[1,4,512,64]{2,3,1,0:T(8,128)S(1)}, u32[]{:S(2)}) copy-start(f32[1,4,512,64]{2,3,1,0:T(8,128)S(1)} %dynamic_update_slice.9) | copy-start | bytes 1572868
  423.6 29.7 %copy-start.7 = (f32[2,4,128,64]{2,3,1,0:T(8,128)S(1)}, f32[2,4,128,64]{2,3,1,0:T(8,128)}, u32[]{:S(2)}) copy-start(f32[2,4,128,64]{2,3,1,0:T(8,128)} %param.16) | copy-start | bytes 786436
  461.4 233.4 %reduce-scatter.2.cloned.1.call-start = ((), (), s32[]{:S(2)}) async-start(), calls=%async_computation.5 | async-start | bytes 2359296 | tf_op jit(solution)/shard_map/reduce_scatter | solution.py:107
  596.9 30.9 %copy-start.8 = (f32[1,4,512,64]{2,3,1,0:T(8,128)S(1)}, f32[1,4,512,64]{2,3,1,0:T(8,128)}, u32[]{:S(2)}) copy-start(f32[1,4,512,64]{2,3,1,0:T(8,128)} %get-tuple-element.25) | copy-start | bytes 1572868
  627.6 264.4 %all-gather.11.cloned.1.call-start = ((), (), s32[]{:S(2)}) async-start(), calls=%async_computation.4 | async-start | bytes 34603008 | tf_op jit(solution)/shard_map/all_gather | solution.py:127
  659.3 1.0 copy-start.2
  904.5 3.4 copy-start.3
  907.9 31.7 %copy-start.4 = (f32[1,4,512,64]{2,3,0,1:T(8,128)S(1)}, f32[1,4,512,64]{2,3,0,1:T(8,128)}, u32[]{:S(2)}) copy-start(f32[1,4,512,64]{2,3,0,1:T(8,128)} %get-tuple-element.27) | copy-start | bytes 1572868
  907.9 31.7 %copy-start.5 = (f32[1,4,512,64]{2,3,0,1:T(8,128)S(1)}, f32[1,4,512,64]{2,3,0,1:T(8,128)}, u32[]{:S(2)}) copy-start(f32[1,4,512,64]{2,3,0,1:T(8,128)} %get-tuple-element.28) | copy-start | bytes 1572868
  911.7 29.6 %copy-start.1 = (f32[8192,64]{0,1:T(8,128)S(1)}, f32[8192,64]{0,1:T(8,128)}, u32[]{:S(2)}) copy-start(f32[8192,64]{0,1:T(8,128)} %param.21) | copy-start | bytes 6291460
Sparse Core Ops, SparseCore 0:
  10.5 27.0 all-gather.6
  39.7 19.8 all-gather.4
  61.1 362.4 all-gather.8
  461.5 130.0 all-reduce.2
  627.8 66.9 reduce-scatter.1
  698.0 193.9 all-gather.10
